TPU v7x, 32 devices: a whole 2x2x4 slice. The times are simulated.
32 devices in a mesh: dp: 8 (over z, y), mp: 4 (over x, core).
Axes of the slice: x: 2, y: 2, z: 4, core: 2. Of those that a mesh axis runs over, the one named last changes fastest.
Arguments:
- tokens: bfloat16 [128, 147, 768], P('dp'), may hold values from -6 to 6
- cotangent: bfloat16 [128, 147, 768], P('dp'), may hold values from -6 to 6
- visible: int32 [128, 147], P('dp'), may hold values from 0 to 587, as said below
- tile_counts: int32 [8], P('dp'), may hold values from 1 to 16, as said below
- attend_weight: float32 [768, 3, 768], P('dp', None, 'mp'), may hold values from -0.3125 to 0.3125
- project_weight: float32 [768, 768], P('mp', 'dp'), may hold values from -0.875 to 0.875
- widen_weight: float32 [768, 3072], P('dp', 'mp'), may hold values from -0.21875 to 0.21875
- narrow_weight: float32 [3072, 768], P('mp', 'dp'), may hold values from -0.109375 to 0.109375
- heads_offset: float32 [2, 12, 64], P(None, 'mp', 'dp'), may hold values from -0.6 to 0.6
- hidden_offset: float32 [48, 64], P('mp', 'dp'), may hold values from -0.6 to 0.6
- layer_vectors: float32 [6, 768], P(None, 'dp'), may hold values from -1 to 2
- attend_first: float32 [768, 3, 768], P('dp', None, 'mp')
- project_first: float32 [768, 768], P('mp', 'dp')
- widen_first: float32 [768, 3072], P('dp', 'mp')
- narrow_first: float32 [3072, 768], P('mp', 'dp')
- heads_first: float32 [2, 12, 64], P(None, 'mp', 'dp')
- hidden_first: float32 [48, 64], P('mp', 'dp')
- vectors_first: float32 [6, 768], P(None, 'dp')
- attend_second: float32 [768, 3, 768], P('dp', None, 'mp')
- project_second: float32 [768, 768], P('mp', 'dp')
- widen_second: float32 [768, 3072], P('dp', 'mp')
- narrow_second: float32 [3072, 768], P('mp', 'dp')
- heads_second: float32 [2, 12, 64], P(None, 'mp', 'dp')
- hidden_second: float32 [48, 64], P('mp', 'dp')
- vectors_second: float32 [6, 768], P(None, 'dp')
Outputs:
- output: bfloat16 [128, 147, 768], P('dp')
- input_grad: float32 [128, 147, 768], P('dp')
- grad_attend: float32 [768, 3, 768], P('dp', None, 'mp')
- grad_project: float32 [768, 768], P('mp', 'dp')
- grad_widen: float32 [768, 3072], P('dp', 'mp')
- grad_narrow: float32 [3072, 768], P('mp', 'dp')
- grad_heads: float32 [2, 12, 64], P(None, 'mp', 'dp')
- grad_hidden: float32 [48, 64], P('mp', 'dp')
- grad_vectors: float32 [6, 768], P(None, 'dp')
- new_attend: float32 [768, 3, 768], P('dp', None, 'mp')
- new_project: float32 [768, 768], P('mp', 'dp')
- new_widen: float32 [768, 3072], P('dp', 'mp')
- new_narrow: float32 [3072, 768], P('mp', 'dp')
- new_heads: float32 [2, 12, 64], P(None, 'mp', 'dp')
- new_hidden: float32 [48, 64], P('mp', 'dp')
- new_vectors: float32 [6, 768], P(None, 'dp')
- first_attend: float32 [768, 3, 768], P('dp', None, 'mp')
- first_project: float32 [768, 768], P('mp', 'dp')
- first_widen: float32 [768, 3072], P('dp', 'mp')
- first_narrow: float32 [3072, 768], P('mp', 'dp')
- first_heads: float32 [2, 12, 64], P(None, 'mp', 'dp')
- first_hidden: float32 [48, 64], P('mp', 'dp')
- first_vectors: float32 [6, 768], P(None, 'dp')
- second_attend: float32 [768, 3, 768], P('dp', None, 'mp')
- second_project: float32 [768, 768], P('mp', 'dp')
- second_widen: float32 [768, 3072], P('dp', 'mp')
- second_narrow: float32 [3072, 768], P('mp', 'dp')
- second_heads: float32 [2, 12, 64], P(None, 'mp', 'dp')
- second_hidden: float32 [48, 64], P('mp', 'dp')
- second_vectors: float32 [6, 768], P(None, 'dp')
- copy_attend: bfloat16 [768, 3, 768], P('dp', None, 'mp')
- copy_project: bfloat16 [768, 768], P('mp', 'dp')
- copy_widen: bfloat16 [768, 3072], P('dp', 'mp')
- copy_narrow: bfloat16 [3072, 768], P('mp', 'dp')
- copy_heads: bfloat16 [2, 12, 64], P(None, 'mp', 'dp')
- copy_hidden: bfloat16 [48, 64], P('mp', 'dp')
- copy_vectors: bfloat16 [6, 768], P(None, 'dp')
Inputs may be any that keep to these rules, and one draw needn't show every extreme that they name: `visible`: the 147 places of one tile are distinct, of 3 frames of 14 x 14 patches. `tile_counts`: slots from this count on hold padding; some device has every slot live and some has one.
All inputs are finite; a program needn't handle non-finite values.
Results may differ from a plain program's by a relative error of at most 0.017.
The roundings to bfloat16 on the way count: a program that leaves them out, or rounds other values in their place, can miss the bound.
Values may be sent and summed in bfloat16 or wider, within the bound.
A program may use at most 192 MiB of HBM per device.

v0:
```python
import math
import jax
import jax.numpy as jnp
from jax import lax
from jax.sharding import PartitionSpec as P

D = 768
FF = 3072
GRID = 14
STEP = 3
LN_EPS = 1e-06
BETA_ONE = 0.5
BETA_TWO = 0.5
ADAM_EPS = 1e-08
DECAY = 0.05


def cut_along(x, dim, size):
    dims = x.shape
    parts = x.reshape(*dims[:dim], size, dims[dim] // size, *dims[dim + 1 :])
    return jnp.moveaxis(parts, dim, 0)


def summed_on_arrival(x, axis, dim):
    size = lax.axis_size(axis)
    parts = lax.all_to_all(cut_along(x, dim, size), axis, 0, 0, tiled=True)
    return jnp.sum(parts.astype(jnp.float32), axis=0)


def sine_table(places, feature_width):
    half_width = feature_width // 2
    spread = jnp.arange(half_width, dtype=jnp.float32) / half_width
    frequency = jnp.exp(-math.log(10000.0) * spread)
    angles = places[..., None] * frequency
    return jnp.concatenate([jnp.sin(angles), jnp.cos(angles)], axis=-1)


def position_table(visible, feature_width):
    plane_size = GRID * GRID
    frame_place = (visible // plane_size).astype(jnp.float32)
    within = visible % plane_size
    row_place = (within // GRID).astype(jnp.float32)
    column_place = (within % GRID).astype(jnp.float32)
    time_width = feature_width // 16 * 4
    space_width = feature_width // 16 * 6
    return jnp.concatenate(
        [
            sine_table(frame_place, time_width),
            sine_table(row_place, space_width),
            sine_table(column_place, space_width),
        ],
        axis=-1,
    )


def normalize(values):
    center = values - jnp.mean(values, axis=-1, keepdims=True)
    inverse = lax.rsqrt(jnp.mean(center * center, axis=-1, keepdims=True) + LN_EPS)
    return (center * inverse, inverse)


def norm_back(grad_normed, normed, inverse):
    return inverse * (
        grad_normed
        - jnp.mean(grad_normed, axis=-1, keepdims=True)
        - normed * jnp.mean(grad_normed * normed, axis=-1, keepdims=True)
    )


def over_rows(former, latter):
    return lax.dot_general(
        former, latter, (((0,), (0,)), ((), ())), preferred_element_type=jnp.float32
    )


def over_cols(former, latter):
    return lax.dot_general(
        former, latter, (((1,), (1,)), ((), ())), preferred_element_type=jnp.float32
    )


def exact_gelu(values):
    return jax.nn.gelu(values, approximate=False)


def adamw_update(
    master, first_moment, second_moment, gradient, step_rate, weight_decay, correction
):
    first_new = BETA_ONE * first_moment + (1.0 - BETA_ONE) * gradient
    second_new = BETA_TWO * second_moment + (1.0 - BETA_TWO) * gradient * gradient
    ratio = first_new / correction / (jnp.sqrt(second_new / correction) + ADAM_EPS)
    master_new = master - step_rate * (ratio + weight_decay * master)
    return (master_new, first_new, second_new)


def shards(
    tokens,
    cotangent,
    visible,
    tile_counts,
    attend_weight,
    project_weight,
    widen_weight,
    narrow_weight,
    heads_offset,
    hidden_offset,
    layer_vectors,
    attend_first,
    project_first,
    widen_first,
    narrow_first,
    heads_first,
    hidden_first,
    vectors_first,
    attend_second,
    project_second,
    widen_second,
    narrow_second,
    heads_second,
    hidden_second,
    vectors_second,
):
    fore_attend, fore_project, fore_widen, fore_narrow, fore_heads, fore_hidden, fore_vectors = (
        lax.all_gather(attend_weight.astype(jnp.bfloat16), "dp", axis=0, tiled=True),
        lax.all_gather(project_weight.astype(jnp.bfloat16), "dp", axis=1, tiled=True),
        lax.all_gather(widen_weight.astype(jnp.bfloat16), "dp", axis=0, tiled=True),
        lax.all_gather(narrow_weight.astype(jnp.bfloat16), "dp", axis=1, tiled=True),
        lax.all_gather(heads_offset.astype(jnp.bfloat16), "dp", axis=2, tiled=True),
        lax.all_gather(hidden_offset.astype(jnp.bfloat16), "dp", axis=1, tiled=True),
        lax.all_gather(layer_vectors.astype(jnp.bfloat16), "dp", axis=1, tiled=True),
    )
    tile_count, seq_length, model_width = tokens.shape
    row_count = tile_count * seq_length
    local_width = fore_attend.shape[2]
    heads_local = fore_heads.shape[1]
    head_size = fore_heads.shape[2]
    score_scale = 1.0 / math.sqrt(head_size)
    live_tiles = (jnp.arange(tile_count, dtype=jnp.int32) < tile_counts[0]).astype(jnp.float32)
    live_rows = jnp.broadcast_to(live_tiles[:, None], (tile_count, seq_length)).reshape(
        row_count, 1
    )
    vectors = fore_vectors.astype(jnp.float32)
    summed = (tokens.astype(jnp.float32) + position_table(visible, model_width)).reshape(
        row_count, model_width
    )
    normed_one, inverse_one = normalize(summed)
    attend_low = (normed_one * vectors[0] + vectors[1]).astype(jnp.bfloat16)
    linear = jnp.dot(
        attend_low,
        fore_attend.reshape(model_width, 3 * local_width),
        preferred_element_type=jnp.float32,
    ).reshape(row_count, 3, local_width)
    offsets = fore_heads.astype(jnp.float32).reshape(2, local_width)
    head_shape = (tile_count, seq_length, heads_local, head_size)
    query_low = (linear[:, 0] + offsets[0]).astype(jnp.bfloat16).reshape(head_shape)
    key_low = linear[:, 1].astype(jnp.bfloat16).reshape(head_shape)
    value_low = (linear[:, 2] + offsets[1]).astype(jnp.bfloat16).reshape(head_shape)
    scores = (
        jnp.einsum("tqhd,tkhd->thqk", query_low, key_low, preferred_element_type=jnp.float32)
        * score_scale
    )
    row_top = jnp.max(scores, axis=-1, keepdims=True)
    log_total = row_top + jnp.log(jnp.sum(jnp.exp(scores - row_top), axis=-1, keepdims=True))
    weights_low = jnp.exp(scores - log_total).astype(jnp.bfloat16)
    context = jnp.einsum(
        "thqk,tkhd->tqhd", weights_low, value_low, preferred_element_type=jnp.float32
    )
    context_low = context.reshape(row_count, local_width).astype(jnp.bfloat16)
    attention_part = jnp.dot(context_low, fore_project, preferred_element_type=jnp.float32)
    attention = lax.psum(attention_part.astype(jnp.bfloat16), "mp").astype(jnp.float32)
    middle = summed + attention + vectors[4]
    normed_two, inverse_two = normalize(middle)
    widen_low = (normed_two * vectors[2] + vectors[3]).astype(jnp.bfloat16)
    hidden = jnp.dot(
        widen_low, fore_widen, preferred_element_type=jnp.float32
    ) + fore_hidden.astype(jnp.float32).reshape(-1)
    active_low = exact_gelu(hidden).astype(jnp.bfloat16)
    feed_part = jnp.dot(active_low, fore_narrow, preferred_element_type=jnp.float32)
    feed_sum = lax.psum(feed_part.astype(jnp.bfloat16), "mp").astype(jnp.float32)
    result = (middle + feed_sum + vectors[5]) * live_rows
    output_low = result.astype(jnp.bfloat16)
    back_attend, back_project, back_widen, back_narrow, back_vectors = (
        fore_attend,
        fore_project,
        fore_widen,
        fore_narrow,
        fore_vectors,
    )
    vectors_back = back_vectors.astype(jnp.float32)
    grad_out = cotangent.astype(jnp.float32).reshape(row_count, model_width) * live_rows
    grad_out_low = grad_out.astype(jnp.bfloat16)
    grad_narrow = over_rows(active_low, grad_out_low)
    grad_active = over_cols(grad_out_low, back_narrow)
    gelu_back = jax.vjp(exact_gelu, hidden)[1]
    grad_hidden_low = gelu_back(grad_active)[0].astype(jnp.bfloat16)
    grad_widen = over_rows(widen_low, grad_hidden_low)
    grad_hidden = jnp.sum(grad_hidden_low.astype(jnp.float32), axis=0).reshape(fore_hidden.shape)
    normed_two_part = over_cols(grad_hidden_low, back_widen)
    grad_normed_two = lax.psum(normed_two_part.astype(jnp.bfloat16), "mp").astype(jnp.float32)
    grad_middle = grad_out + norm_back(grad_normed_two * vectors_back[2], normed_two, inverse_two)
    grad_middle_low = grad_middle.astype(jnp.bfloat16)
    grad_project = over_rows(context_low, grad_middle_low)
    grad_context_low = (
        over_cols(grad_middle_low, back_project).astype(jnp.bfloat16).reshape(head_shape)
    )
    scores_again = (
        jnp.einsum("tqhd,tkhd->thqk", query_low, key_low, preferred_element_type=jnp.float32)
        * score_scale
    )
    weights_full = jnp.exp(scores_again - log_total)
    weights_again_low = weights_full.astype(jnp.bfloat16)
    grad_weights = jnp.einsum(
        "tqhd,tkhd->thqk", grad_context_low, value_low, preferred_element_type=jnp.float32
    )
    grad_value = jnp.einsum(
        "thqk,tqhd->tkhd", weights_again_low, grad_context_low, preferred_element_type=jnp.float32
    )
    row_dot = jnp.sum(grad_weights * weights_full, axis=-1, keepdims=True)
    grad_scores_low = (weights_full * (grad_weights - row_dot)).astype(jnp.bfloat16)
    grad_query = (
        jnp.einsum("thqk,tkhd->tqhd", grad_scores_low, key_low, preferred_element_type=jnp.float32)
        * score_scale
    )
    grad_key = (
        jnp.einsum(
            "thqk,tqhd->tkhd", grad_scores_low, query_low, preferred_element_type=jnp.float32
        )
        * score_scale
    )
    grad_qkv_low = jnp.stack(
        [
            grad_query.reshape(row_count, local_width),
            grad_key.reshape(row_count, local_width),
            grad_value.reshape(row_count, local_width),
        ],
        axis=1,
    ).astype(jnp.bfloat16)
    grad_offsets = jnp.sum(grad_qkv_low.astype(jnp.float32), axis=0)
    grad_heads = jnp.stack([grad_offsets[0], grad_offsets[2]]).reshape(2, heads_local, head_size)
    flat_qkv = grad_qkv_low.reshape(row_count, 3 * local_width)
    grad_attend = over_rows(attend_low, flat_qkv).reshape(model_width, 3, local_width)
    normed_one_part = over_cols(flat_qkv, back_attend.reshape(model_width, 3 * local_width))
    grad_normed_one = lax.psum(normed_one_part.astype(jnp.bfloat16), "mp").astype(jnp.float32)
    grad_inputs = grad_middle + norm_back(
        grad_normed_one * vectors_back[0], normed_one, inverse_one
    )
    grad_vectors = jnp.stack(
        [
            jnp.sum(grad_normed_one * normed_one, axis=0),
            jnp.sum(grad_normed_one, axis=0),
            jnp.sum(grad_normed_two * normed_two, axis=0),
            jnp.sum(grad_normed_two, axis=0),
            jnp.sum(grad_middle, axis=0),
            jnp.sum(grad_out, axis=0),
        ]
    )
    output = output_low.reshape(tile_count, seq_length, model_width)
    input_grad = grad_inputs.reshape(tile_count, seq_length, model_width)
    (
        shard_attend,
        shard_project,
        shard_widen,
        shard_narrow,
        shard_heads,
        shard_hidden,
        shard_vectors,
    ) = (
        summed_on_arrival(grad_attend.astype(jnp.bfloat16), "dp", 0),
        summed_on_arrival(grad_project.astype(jnp.bfloat16), "dp", 1),
        summed_on_arrival(grad_widen.astype(jnp.bfloat16), "dp", 0),
        summed_on_arrival(grad_narrow.astype(jnp.bfloat16), "dp", 1),
        summed_on_arrival(grad_heads.astype(jnp.bfloat16), "dp", 2),
        summed_on_arrival(grad_hidden.astype(jnp.bfloat16), "dp", 1),
        summed_on_arrival(grad_vectors.astype(jnp.bfloat16), "dp", 1),
    )
    correction = 1.0 - 0.5**STEP
    new_attend, first_attend, second_attend = adamw_update(
        attend_weight,
        attend_first,
        attend_second,
        shard_attend,
        (D // 2) ** (-0.5),
        DECAY,
        correction,
    )
    new_project, first_project, second_project = adamw_update(
        project_weight,
        project_first,
        project_second,
        shard_project,
        (D // 16) ** (-0.5),
        DECAY,
        correction,
    )
    new_widen, first_widen, second_widen = adamw_update(
        widen_weight, widen_first, widen_second, shard_widen, D ** (-0.5), DECAY, correction
    )
    new_narrow, first_narrow, second_narrow = adamw_update(
        narrow_weight, narrow_first, narrow_second, shard_narrow, FF ** (-0.5), DECAY, correction
    )
    new_heads, first_heads, second_heads = adamw_update(
        heads_offset, heads_first, heads_second, shard_heads, 0.1, 0.0, correction
    )
    new_hidden, first_hidden, second_hidden = adamw_update(
        hidden_offset, hidden_first, hidden_second, shard_hidden, 0.1, 0.0, correction
    )
    new_vectors, first_vectors, second_vectors = adamw_update(
        layer_vectors, vectors_first, vectors_second, shard_vectors, 0.15, 0.0, correction
    )
    return (
        output,
        input_grad,
        shard_attend,
        shard_project,
        shard_widen,
        shard_narrow,
        shard_heads,
        shard_hidden,
        shard_vectors,
        new_attend,
        new_project,
        new_widen,
        new_narrow,
        new_heads,
        new_hidden,
        new_vectors,
        first_attend,
        first_project,
        first_widen,
        first_narrow,
        first_heads,
        first_hidden,
        first_vectors,
        second_attend,
        second_project,
        second_widen,
        second_narrow,
        second_heads,
        second_hidden,
        second_vectors,
        new_attend.astype(jnp.bfloat16),
        new_project.astype(jnp.bfloat16),
        new_widen.astype(jnp.bfloat16),
        new_narrow.astype(jnp.bfloat16),
        new_heads.astype(jnp.bfloat16),
        new_hidden.astype(jnp.bfloat16),
        new_vectors.astype(jnp.bfloat16),
    )


def solution(mesh):
    in_specs = (
        P("dp", None, None),
        P("dp", None, None),
        P("dp", None),
        P("dp"),
        P("dp", None, "mp"),
        P("mp", "dp"),
        P("dp", "mp"),
        P("mp", "dp"),
        P(None, "mp", "dp"),
        P("mp", "dp"),
        P(None, "dp"),
        P("dp", None, "mp"),
        P("mp", "dp"),
        P("dp", "mp"),
        P("mp", "dp"),
        P(None, "mp", "dp"),
        P("mp", "dp"),
        P(None, "dp"),
        P("dp", None, "mp"),
        P("mp", "dp"),
        P("dp", "mp"),
        P("mp", "dp"),
        P(None, "mp", "dp"),
        P("mp", "dp"),
        P(None, "dp"),
    )
    out_specs = (
        P("dp", None, None),
        P("dp", None, None),
        P("dp", None, "mp"),
        P("mp", "dp"),
        P("dp", "mp"),
        P("mp", "dp"),
        P(None, "mp", "dp"),
        P("mp", "dp"),
        P(None, "dp"),
        P("dp", None, "mp"),
        P("mp", "dp"),
        P("dp", "mp"),
        P("mp", "dp"),
        P(None, "mp", "dp"),
        P("mp", "dp"),
        P(None, "dp"),
        P("dp", None, "mp"),
        P("mp", "dp"),
        P("dp", "mp"),
        P("mp", "dp"),
        P(None, "mp", "dp"),
        P("mp", "dp"),
        P(None, "dp"),
        P("dp", None, "mp"),
        P("mp", "dp"),
        P("dp", "mp"),
        P("mp", "dp"),
        P(None, "mp", "dp"),
        P("mp", "dp"),
        P(None, "dp"),
        P("dp", None, "mp"),
        P("mp", "dp"),
        P("dp", "mp"),
        P("mp", "dp"),
        P(None, "mp", "dp"),
        P("mp", "dp"),
        P(None, "dp"),
    )
    return jax.shard_map(shards, mesh=mesh, in_specs=in_specs, out_specs=out_specs, check_vma=False)
```

profile of v0, /device:TPU:0, one launch (start us, length us, event | category | flops | bytes accessed | tf_op | source)
XLA Modules:
  0.0 817.2 jit_solution(17125010776778953683)
XLA Ops:
  8.8 27.9 %all-gather = bf16[8,96,6]{1,2,0:T(8,128)(2,1)S(1)} all-gather(bf16[1,96,6]{1,2,0:T(8,128)(2,1)S(1)} %convert_bitcast_fusion), channel_id=1, replica_groups=mesh['dp'=8,'mp'=4] {'dp'}, dimensions={0}, use_global_device_ids=true | all-gather | bytes 10368 | tf_op jit(solution)/shard_map/all_gather | solution.py:130
  39.5 33.2 %all_gather.22 = bf16[768,3,192]{2,0,1:T(8,128)(2,1)S(1)} all-gather(bf16[96,3,192]{2,0,1:T(8,128)(2,1)S(1)} %convert_element_type.217), channel_id=1, replica_groups=mesh['dp'=8,'mp'=4] {'dp'}, dimensions={0}, use_global_device_ids=true | all-gather | bytes 995328 | tf_op jit(solution)/shard_map/all_gather | solution.py:124
  73.7 5.7 multiply_cosine_fusion.2
  79.4 19.3 %multiply_cosine_fusion = (f32[16,147,144]{2,0,1:T(8,128)S(1)}, f32[16,147,144]{2,0,1:T(8,128)}, f32[16,147,144]{2,0,1:T(8,128)}, f32[16,147,144]{2,0,1:T(8,128)}) fusion(f32[16,147]{0,1:T(8,128)S(1)} %copy.347, f32[144]{0:T(256)S(1)} %multiply_exponential_fusion, f32[16,147]{0,1:T(8,128)S(1)} %copy.346), kind=kLoop, calls=%fused_computation.60 | loop fusion | flops 677376 | bytes 5438400 | tf_op jit(solution)/shard_map/cos | solution.py:35
  98.7 11.6 %concatenate.5 = f32[16,147,768]{2,0,1:T(8,128)} concatenate(f32[16,147,96]{2,0,1:T(8,128)} %get-tuple-element.356, f32[16,147,96]{2,0,1:T(8,128)} %get-tuple-element.355, f32[16,147,144]{2,0,1:T(8,128)} %get-tuple-element.364, f32[16,147,144]{2,0,1:T(8,128)} %get-tuple-element.365, f32[16,147,144]{2,0,1:T(8,128)} %get-tuple-element.352, f32[16,147,144]{2,0,1:T(8,128)S(1)} %get-tuple-element.351), dimensions={2} | concatenate | bytes 14450688 | tf_op jit(solution)/shard_map/concatenate | solution.py:46
  110.3 7.8 fusion.87
  118.8 4.0 multiply_reduce_fusion.3
  123.0 3.8 add_convert_fusion.2
  126.8 3.1 copy.354
  129.9 3.9 reshape.315
  133.8 4.5 fusion.43
  140.7 30.6 %all_gather.23 = bf16[2,3,64]{1,0,2:T(2,128)(2,1)S(1)} all-gather(bf16[2,3,8]{1,0,2:T(2,128)(2,1)S(1)} %copy.356), channel_id=1, replica_groups=mesh['dp'=8,'mp'=4] {'dp'}, dimensions={2}, use_global_device_ids=true | all-gather | bytes 864 | tf_op jit(solution)/shard_map/all_gather | solution.py:128
  171.6 31.4 %all_gather.24 = bf16[192,768]{0,1:T(8,128)(2,1)S(1)} all-gather(bf16[192,96]{0,1:T(8,128)(2,1)S(1)} %copy.364), channel_id=1, replica_groups=mesh['dp'=8,'mp'=4] {'dp'}, dimensions={1}, use_global_device_ids=true | all-gather | bytes 331776 | tf_op jit(solution)/shard_map/all_gather | solution.py:125
  202.9 5.3 convert_element_type.222
  208.2 5.4 squeeze.10
  213.6 6.2 squeeze.11
  219.8 5.9 multiply_reduce_fusion.4
  228.7 3.1 fusion.30
  233.9 4.0 convert_element_type.226
  237.9 4.2 convolution_convert_fusion.2
  243.8 12.3 %all-gather.6.cloned.1.call-start = ((), (), s32[]{:S(2)}) async-start(), calls=%async_computation.9 | async-start | bytes 1327104 | tf_op jit(solution)/shard_map/all_gather | solution.py:127
  256.1 10.4 %copy.348 = f32[16,147,768]{2,1,0:T(8,128)} copy(f32[16,147,768]{2,0,1:T(8,128)} %get-tuple-element.347) | data formatting | bytes 14450688 | tf_op jit(solution)/shard_map/add | solution.py:143
  267.7 26.3 %all_gather.26 = bf16[12,64]{0,1:T(8,128)(2,1)S(1)} all-gather(bf16[12,8]{0,1:T(8,128)(2,1)S(1)} %convert_element_type.232), channel_id=1, replica_groups=mesh['dp'=8,'mp'=4] {'dp'}, dimensions={1}, use_global_device_ids=true | all-gather | bytes 1728 | tf_op jit(solution)/shard_map/all_gather | solution.py:129
  297.5 6.2 copy.366
  303.7 5.5 reshape.304
  309.2 5.6 reshape.301
  314.8 3.8 all-reduce.5.cloned.1.call-done
  318.6 5.1 fusion.86
  329.4 21.0 %multiply_convert_fusion.2 = (bf16[2352,768]{1,0:T(8,128)(2,1)S(1)}, f32[2352,768]{1,0:T(8,128)}, f32[2352,768]{1,0:T(8,128)}) fusion(f32[768]{0:T(1024)} %reshape.311, bf16[2352,768]{1,0:T(8,128)(2,1)} %add_convert_fusion.1, bf16[768,768]{1,0:T(8,128)(2,1)} %all-gather.4.cloned.1.call-done), kind=kOutput, calls=%fused_computation.31 | convolution fusion | flops 2893750272 | bytes 22858752 | tf_op jit(solution)/shard_map/dot_general | solution.py:174
  350.4 7.9 convolution_convert_fusion.5
  358.3 34.1 %all_to_all.35 = bf16[8,768,96]{1,2,0:T(8,128)(2,1)S(1)} all-to-all(bf16[8,768,96]{1,2,0:T(8,128)(2,1)S(1)} %bitcast.97), channel_id=1, replica_groups=mesh['dp'=8,'mp'=4] {'dp'}, dimensions={0} | all-to-all | bytes 2359296 | tf_op jit(solution)/shard_map/all_to_all | solution.py:26
  394.6 39.3 %all-gather.6.cloned.1.call-done = bf16[768,768]{0,1:T(8,128)(2,1)} async-done(((bf16[768,96]{0,1:T(8,128)(2,1)}), bf16[768,768]{0,1:T(8,128)(2,1)}) %all-gather.6.cloned.1.call-update) | async-done | bytes 1179664 | tf_op jit(solution)/shard_map/all_gather | solution.py:127
  433.9 11.3 %fusion.91 = (bf16[768]{0:T(1024)(128)(2,1)}, bf16[2352,768]{1,0:T(8,128)(2,1)S(1)}) fusion(f32[2352,768]{1,0:T(8,128)} %get-tuple-element.343, bf16[768,768]{0,1:T(8,128)(2,1)} %all-gather.6.cloned.1.call-done, f32[2352,768]{1,0:T(8,128)} %reshape.304, f32[2352]{0:T(1024)} %mul.444, f32[2352,768]{1,0:T(8,128)} %get-tuple-element.368, f32[768]{0:T(1024)} %reshape.311), kind=kOutput, calls=%fused_computation.191 | convolution fusion | flops 2807045376 | bytes 26482368 | tf_op jit(solution)/shard_map/dot_general | solution.py:77
  447.0 4.5 convolution_convert_fusion
  454.4 3.9 all-to-all-start.5
  458.3 68.1 %all-reduce.7.cloned.1.call-done = bf16[2352,768]{1,0:T(8,128)(2,1)} async-done(((bf16[2352,768]{1,0:T(8,128)(2,1)}), bf16[2352,768]{1,0:T(8,128)(2,1)}) %all-reduce.7.cloned.1.call-update) | async-done | bytes 3612688 | tf_op jit(solution)/shard_map/psum | solution.py:199
  526.4 7.8 fusion.10
  534.2 7.6 fusion.82
  546.9 6.2 reshape.305
  553.1 5.6 convolution_bitcast_fusion
  558.7 7.2 multiply_reduce_fusion
  573.5 3.0 stack_reshape.11
  578.7 3.0 stack_reshape.9
  584.7 3.4 fusion.84
  588.9 5.8 all-to-all-start.4
  594.6 7.5 convolution_convert_fusion.6
  602.1 6.0 all-to-all-start.2
  608.2 7.3 convolution_convert_fusion.1
  615.5 4.9 bitcast_convert_fusion
  621.6 4.0 fusion.40
  626.9 9.3 %all-to-all-done.2 = bf16[8,96,768]{2,1,0:T(8,128)(2,1)S(1)} async-done(((bf16[8,96,768]{2,1,0:T(8,128)(2,1)}), bf16[8,96,768]{2,1,0:T(8,128)(2,1)S(1)}, u32[]{:S(2)}, u32[]{:S(2)}) %all-to-all-start.2) | async-done | bytes 1179680 | tf_op jit(solution)/shard_map/all_to_all | solution.py:26
  636.2 3.9 all-to-all-start.1
  640.1 6.4 fusion.31
  651.8 4.4 all-to-all-start
  656.3 3.0 multiply_reduce_fusion.1
  675.7 8.8 %all-to-all-done = bf16[8,96,3,192]{1,3,2,0:T(8,128)(2,1)S(1)} async-done(((bf16[8,96,3,192]{1,3,2,0:T(8,128)(2,1)}), bf16[8,96,3,192]{1,3,2,0:T(8,128)(2,1)S(1)}, u32[]{:S(2)}, u32[]{:S(2)}) %all-to-all-start) | async-done | bytes 884768 | tf_op jit(solution)/shard_map/all_to_all | solution.py:26
  690.4 65.6 %all-reduce.9.cloned.1.call-done = (bf16[2352,768]{1,0:T(8,128)(2,1)}, bf16[2352,768]{1,0:T(8,128)(2,1)}) async-done(((bf16[2352,768]{1,0:T(8,128)(2,1)}, bf16[2352,768]{1,0:T(8,128)(2,1)}), (bf16[2352,768]{1,0:T(8,128)(2,1)}, bf16[2352,768]{1,0:T(8,128)(2,1)})) %all-reduce.9.cloned.1.call-update) | async-done | bytes 7225360 | tf_op jit(solution)/shard_map/psum | solution.py:179
  758.7 7.2 fusion.15
  766.7 5.7 all-to-all-start.6
  772.5 11.5 %fusion.13 = f32[2352,768]{1,0:T(8,128)} fusion(f32[2352,768]{1,0:T(8,128)} %copy-done.2, bf16[2352,768]{1,0:T(8,128)(2,1)} %get-tuple-element.309, f32[2352,768]{1,0:T(8,128)} %reshape.301, f32[2352]{0:T(1024)S(1)} %broadcast_multiply_fusion.1, f32[2352]{0:T(1024)S(1)} %div.112, f32[2352]{0:T(1024)S(1)} %broadcast_multiply_fusion.2, f32[768]{0:T(1024)S(1)} %copy-done.35, ...), kind=kLoop, calls=%fused_computation.22 | loop fusion | flops 16257024 | bytes 25329408 | tf_op jit(solution)/shard_map/add | solution.py:244
  786.9 3.8 reshape.303
  790.7 4.6 copy.395
  795.3 5.4 reshape.306
  800.7 8.5 %copy.396 = f32[16,147,768]{2,0,1:T(8,128)} copy(f32[16,147,768]{2,1,0:T(8,128)} %reshape.306) | data formatting | bytes 14450688
  (256 shorter events, 86.7 us)
Async XLA Ops:
  8.0 310.5 %all-reduce.5.cloned.1.call-start = ((), (), s32[]{:S(2)}) async-start(), calls=%async_computation.7 | async-start | bytes 7225344 | tf_op jit(solution)/shard_map/psum | solution.py:170
  37.5 85.6 %copy-start.34 = (f32[768]{0:T(1024)}, f32[768]{0:T(1024)S(1)}, u32[]{:S(2)}) copy-start(f32[768]{0:T(1024)S(1)} %get-tuple-element.307) | copy-start | bytes 9220
  122.9 7.0 copy-start.27
  138.3 33.1 %copy-start.17 = (f32[192,96]{1,0:T(8,128)S(1)}, f32[192,96]{1,0:T(8,128)}, u32[]{:S(2)}) copy-start(f32[192,96]{1,0:T(8,128)} %param.30) | copy-start | bytes 221188
  171.4 56.1 %copy-start.39 = (f32[1,3,64]{2,1,0:T(4,128)}, f32[1,3,64]{2,1,0:T(4,128)S(1)}, u32[]{:S(2)}) copy-start(f32[1,3,64]{2,1,0:T(4,128)S(1)} %copy.357) | copy-start | bytes 2308
  171.5 54.3 %copy-start.37 = (f32[1,3,64]{2,1,0:T(4,128)}, f32[1,3,64]{2,1,0:T(4,128)S(1)}, u32[]{:S(2)}) copy-start(f32[1,3,64]{2,1,0:T(4,128)S(1)} %copy.359) | copy-start | bytes 2308
  225.8 6.1 copy-start
  242.1 87.3 %all-gather.4.cloned.1.call-start = ((), (), s32[]{:S(2)}) async-start(), calls=%async_computation.8 | async-start | bytes 1327104 | tf_op jit(solution)/shard_map/all_gather | solution.py:126
  243.8 23.9 %copy-start.46 = (f32[12,8]{0,1:T(8,128)S(1)}, f32[12,8]{0,1:T(8,128)}, u32[]{:S(2)}) copy-start(f32[12,8]{0,1:T(8,128)} %param.34) | copy-start | bytes 1156
  243.8 190.0 %all-gather.6.cloned.1.call-start = ((), (), s32[]{:S(2)}) async-start(), calls=%async_computation.9 | async-start | bytes 1327104 | tf_op jit(solution)/shard_map/all_gather | solution.py:127
  309.2 9.3 %copy-start.43 = (f32[768]{0:T(1024)S(1)}, f32[768]{0:T(1024)}, u32[]{:S(2)}) copy-start(f32[768]{0:T(1024)} %get-tuple-element.305) | copy-start | bytes 9220
  323.7 2.9 copy-start.1
  323.7 3.0 copy-start.36
  323.7 3.0 copy-start.42
  329.4 21.0 %copy-start.29 = (f32[2352]{0:T(1024)S(1)}, f32[2352]{0:T(1024)}, u32[]{:S(2)}) copy-start(f32[2352]{0:T(1024)} %mul.444) | copy-start | bytes 28228
  350.4 8.0 copy-start.62
  350.4 42.9 %copy-start.20 = (f32[768,96]{0,1:T(8,128)S(1)}, f32[768,96]{0,1:T(8,128)}, u32[]{:S(2)}) copy-start(f32[768,96]{0,1:T(8,128)} %param.32) | copy-start | bytes 884740
  350.4 42.9 %copy-start.21 = (f32[768,96]{0,1:T(8,128)S(1)}, f32[768,96]{0,1:T(8,128)}, u32[]{:S(2)}) copy-start(f32[768,96]{0,1:T(8,128)} %param.39) | copy-start | bytes 884740
  350.4 42.9 %copy-start.22 = (f32[768,96]{0,1:T(8,128)S(1)}, f32[768,96]{0,1:T(8,128)}, u32[]{:S(2)}) copy-start(f32[768,96]{0,1:T(8,128)} %param.46) | copy-start | bytes 884740
  394.5 131.9 %all-reduce.7.cloned.1.call-start = ((), (), s32[]{:S(2)}) async-start(), calls=%async_computation.10 | async-start | bytes 7225344 | tf_op jit(solution)/shard_map/psum | solution.py:199
  433.9 13.2 %copy-start.60 = (bf16[768,768]{1,0:T(8,128)(2,1)S(1)}, bf16[768,768]{1,0:T(8,128)(2,1)}, u32[]{:S(2)}) copy-start(bf16[768,768]{1,0:T(8,128)(2,1)} %all-gather.4.cloned.1.call-done) | copy-start | bytes 3538948
  454.4 134.5 %all-to-all-start.5 = ((bf16[8,12,8]{1,2,0:T(8,128)(2,1)}), bf16[8,12,8]{1,2,0:T(8,128)(2,1)}, u32[]{:S(2)}, u32[]{:S(2)}) async-start(bf16[8,12,8]{1,2,0:T(8,128)(2,1)} %copy.382), calls=%async_computation.5 | async-start | bytes 32768 | tf_op jit(solution)/shard_map/all_to_all | solution.py:26
  526.4 7.8 copy-start.3
  526.4 7.8 copy-start.24
  526.4 7.8 copy-start.30
  546.9 11.8 %copy-start.13 = (f32[16,3,147]{2,1,0:T(4,128)S(1)}, f32[16,3,147]{2,1,0:T(4,128)}, u32[]{:S(2)}) copy-start(f32[16,3,147]{2,1,0:T(4,128)} %copy-done.12) | copy-start | bytes 84676
  546.9 11.8 %copy-start.40 = (f32[1,3,64]{2,1,0:T(4,128)S(1)}, f32[1,3,64]{2,1,0:T(4,128)}, u32[]{:S(2)}) copy-start(f32[1,3,64]{2,1,0:T(4,128)} %copy-done.39) | copy-start | bytes 2308
  553.1 5.7 copy-start.6
  553.1 12.9 %slice-start = ((s8[7471104]{0:T(1024)(128)(4,1)}), s8[4194304]{0:T(1024)(128)(4,1)S(1)}, s32[]{:S(2)}) async-start(s8[7471104]{0:T(1024)(128)(4,1)} %bitcast.93), calls=%async_computation.12 | async-start | bytes 8388608
  558.7 7.3 slice-start.1
  588.9 13.3 %all-to-all-start.4 = ((bf16[8,2,3,8]{3,1,2,0:T(2,128)(2,1)}), bf16[8,2,3,8]{3,1,2,0:T(2,128)(2,1)S(1)}, u32[]{:S(2)}, u32[]{:S(2)}) async-start(bf16[8,2,3,8]{3,1,2,0:T(2,128)(2,1)} %copy.379), calls=%async_computation.4 | async-start | bytes 24576 | tf_op jit(solution)/shard_map/all_to_all | solution.py:26
  602.1 34.1 %all-to-all-start.2 = ((bf16[8,96,768]{2,1,0:T(8,128)(2,1)}), bf16[8,96,768]{2,1,0:T(8,128)(2,1)S(1)}, u32[]{:S(2)}, u32[]{:S(2)}) async-start(bf16[8,96,768]{2,1,0:T(8,128)(2,1)} %bitcast.18), calls=%async_computation.2 | async-start | bytes 2359296 | tf_op jit(solution)/shard_map/all_to_all | solution.py:26
  608.1 7.4 copy-start.9
  608.2 147.9 %all-reduce.9.cloned.1.call-start = ((), (), s32[]{:S(2)}) async-start(), calls=%async_computation.11 | async-start | bytes 14450688 | tf_op jit(solution)/shard_map/psum | solution.py:179
  608.2 7.3 copy-start.11
  636.2 15.6 %all-to-all-start.1 = ((bf16[8,192,96]{2,1,0:T(8,128)(2,1)}), bf16[8,192,96]{2,1,0:T(8,128)(2,1)S(1)}, u32[]{:S(2)}, u32[]{:S(2)}) async-start(bf16[8,192,96]{2,1,0:T(8,128)(2,1)} %bitcast.91), calls=%async_computation.1 | async-start | bytes 786432 | tf_op jit(solution)/shard_map/all_to_all | solution.py:26
  640.1 16.2 %copy-start.59 = (f32[16]{0:T(128)S(1)}, f32[16]{0:T(128)}, u32[]{:S(2)}) copy-start(f32[16]{0:T(128)} %compare_convert_fusion) | copy-start | bytes 196
  646.5 14.6 %copy-start.26 = (f32[16,147]{1,0:T(8,128)S(1)}, f32[16,147]{1,0:T(8,128)}, u32[]{:S(2)}) copy-start(f32[16,147]{1,0:T(8,128)} %copy-done.25) | copy-start | bytes 28228
  646.5 14.8 %copy-start.28 = (f32[16,147]{1,0:T(8,128)S(1)}, f32[16,147]{1,0:T(8,128)}, u32[]{:S(2)}) copy-start(f32[16,147]{1,0:T(8,128)} %copy-done.27) | copy-start | bytes 28228
  646.5 19.3 %copy-start.47 = (f32[12,8]{0,1:T(8,128)S(1)}, f32[12,8]{0,1:T(8,128)}, u32[]{:S(2)}) copy-start(f32[12,8]{0,1:T(8,128)} %param.34) | copy-start | bytes 1156
  646.5 19.3 %copy-start.53 = (f32[12,8]{0,1:T(8,128)S(1)}, f32[12,8]{0,1:T(8,128)}, u32[]{:S(2)}) copy-start(f32[12,8]{0,1:T(8,128)} %param.41) | copy-start | bytes 1156
  646.5 19.3 %copy-start.54 = (f32[12,8]{0,1:T(8,128)S(1)}, f32[12,8]{0,1:T(8,128)}, u32[]{:S(2)}) copy-start(f32[12,8]{0,1:T(8,128)} %param.48) | copy-start | bytes 1156
  648.9 20.2 %copy-start.51 = (bf16[768]{0:T(1024)(128)(2,1)S(1)}, bf16[768]{0:T(1024)(128)(2,1)}, u32[]{:S(2)}) copy-start(bf16[768]{0:T(1024)(128)(2,1)} %get-tuple-element.296) | copy-start | bytes 4612
  649.0 20.3 %copy-start.52 = (bf16[768]{0:T(1024)(128)(2,1)S(1)}, bf16[768]{0:T(1024)(128)(2,1)}, u32[]{:S(2)}) copy-start(bf16[768]{0:T(1024)(128)(2,1)} %get-tuple-element.338) | copy-start | bytes 4612
  649.0 21.0 %copy-start.50 = (f32[2,3,8]{2,0,1:T(2,128)S(1)}, f32[2,3,8]{2,0,1:T(2,128)}, u32[]{:S(2)}) copy-start(f32[2,3,8]{2,0,1:T(2,128)} %param.33) | copy-start | bytes 580
  649.0 21.0 %copy-start.57 = (f32[2,3,8]{2,0,1:T(2,128)S(1)}, f32[2,3,8]{2,0,1:T(2,128)}, u32[]{:S(2)}) copy-start(f32[2,3,8]{2,0,1:T(2,128)} %param.40) | copy-start | bytes 580
  649.0 21.0 %copy-start.58 = (f32[2,3,8]{2,0,1:T(2,128)S(1)}, f32[2,3,8]{2,0,1:T(2,128)}, u32[]{:S(2)}) copy-start(f32[2,3,8]{2,0,1:T(2,128)} %param.47) | copy-start | bytes 580
  649.0 23.5 %copy-start.14 = (f32[96,768]{1,0:T(8,128)S(1)}, f32[96,768]{1,0:T(8,128)}, u32[]{:S(2)}) copy-start(f32[96,768]{1,0:T(8,128)} %param.31) | copy-start | bytes 884740
  651.8 32.7 %all-to-all-start = ((bf16[8,96,3,192]{1,3,2,0:T(8,128)(2,1)}), bf16[8,96,3,192]{1,3,2,0:T(8,128)(2,1)S(1)}, u32[]{:S(2)}, u32[]{:S(2)}) async-start(bf16[8,96,3,192]{1,3,2,0:T(8,128)(2,1)} %copy.376), calls=%async_computation | async-start | bytes 2359296 | tf_op jit(solution)/shard_map/all_to_all | solution.py:26
  656.2 18.6 %copy-start.18 = (f32[192,96]{1,0:T(8,128)S(1)}, f32[192,96]{1,0:T(8,128)}, u32[]{:S(2)}) copy-start(f32[192,96]{1,0:T(8,128)} %param.30) | copy-start | bytes 221188
  656.3 18.6 %copy-start.32 = (f32[192,96]{1,0:T(8,128)S(1)}, f32[192,96]{1,0:T(8,128)}, u32[]{:S(2)}) copy-start(f32[192,96]{1,0:T(8,128)} %param.37) | copy-start | bytes 221188
  656.3 18.6 %copy-start.33 = (f32[192,96]{1,0:T(8,128)S(1)}, f32[192,96]{1,0:T(8,128)}, u32[]{:S(2)}) copy-start(f32[192,96]{1,0:T(8,128)} %param.44) | copy-start | bytes 221188
  665.9 24.6 %copy-start.44 = (f32[12,8]{0,1:T(8,128)}, f32[12,8]{0,1:T(8,128)S(1)}, u32[]{:S(2)}) copy-start(f32[12,8]{0,1:T(8,128)S(1)} %convert_reduce_fusion.5) | copy-start | bytes 1156
  672.3 86.4 %copy-start.35 = (f32[768]{0:T(1024)S(1)}, f32[768]{0:T(1024)}, u32[]{:S(2)}) copy-start(f32[768]{0:T(1024)} %copy-done.34) | copy-start | bytes 9220
  674.9 91.1 %copy-start.19 = (f32[192,96]{1,0:T(8,128)}, f32[192,96]{1,0:T(8,128)S(1)}, u32[]{:S(2)}) copy-start(f32[192,96]{1,0:T(8,128)S(1)} %convert_reduce_fusion.3) | copy-start | bytes 221188
  758.7 25.3 %slice-start.2 = ((s8[7225344]{0:T(1024)(128)(4,1)}), s8[3031040]{0:T(1024)(128)(4,1)S(1)}, s32[]{:S(2)}) async-start(s8[7225344]{0:T(1024)(128)(4,1)} %bitcast.95), calls=%async_computation.14 | async-start | bytes 6062080
  766.7 42.5 %all-to-all-start.6 = ((bf16[8,6,96]{2,1,0:T(8,128)(2,1)}), bf16[8,6,96]{2,1,0:T(8,128)(2,1)S(1)}, u32[]{:S(2)}, u32[]{:S(2)}) async-start(bf16[8,6,96]{2,1,0:T(8,128)(2,1)} %copy.384), calls=%async_computation.6 | async-start | bytes 32768 | tf_op jit(solution)/shard_map/all_to_all | solution.py:26
  772.4 11.6 %slice-start.3 = ((s8[7225344]{0:T(1024)(128)(4,1)}), s8[4194304]{0:T(1024)(128)(4,1)S(1)}, s32[]{:S(2)}) async-start(s8[7225344]{0:T(1024)(128)(4,1)} %bitcast.95), calls=%async_computation.15 | async-start | bytes 8388608
  772.5 11.6 %copy-start.10 = (bf16[2352,768]{1,0:T(8,128)(2,1)S(1)}, bf16[2352,768]{1,0:T(8,128)(2,1)}, u32[]{:S(2)}) copy-start(bf16[2352,768]{1,0:T(8,128)(2,1)} %get-tuple-element.308) | copy-start | bytes 10838020
  772.5 11.6 %copy-start.31 = (f32[2352]{0:T(1024)S(1)}, f32[2352]{0:T(1024)}, u32[]{:S(2)}) copy-start(f32[2352]{0:T(1024)} %mul.444) | copy-start | bytes 28228
  772.5 11.6 %copy-start.41 = (f32[768]{0:T(1024)S(1)}, f32[768]{0:T(1024)}, u32[]{:S(2)}) copy-start(f32[768]{0:T(1024)} %get-tuple-element.302) | copy-start | bytes 9220
  800.7 8.5 %copy-start.48 = (f32[6,96]{1,0:T(8,128)S(1)}, f32[6,96]{1,0:T(8,128)}, u32[]{:S(2)}) copy-start(f32[6,96]{1,0:T(8,128)} %param.35) | copy-start | bytes 6916
  800.7 8.5 %copy-start.55 = (f32[6,96]{1,0:T(8,128)S(1)}, f32[6,96]{1,0:T(8,128)}, u32[]{:S(2)}) copy-start(f32[6,96]{1,0:T(8,128)} %param.42) | copy-start | bytes 6916
  800.7 8.5 %copy-start.56 = (f32[6,96]{1,0:T(8,128)S(1)}, f32[6,96]{1,0:T(8,128)}, u32[]{:S(2)}) copy-start(f32[6,96]{1,0:T(8,128)} %param.49) | copy-start | bytes 6916
  (14 other events, 22.7 us)
Sparse Core Ops, SparseCore 0:
  242.2 76.3 all-reduce.4
  451.7 74.6 all-reduce.6
  620.6 135.3 all-reduce.8
Sparse Core Ops, SparseCore 1:
  245.3 41.3 all-gather.3
  394.6 39.2 all-gather.5
where the time goes:
time: 827 us; the launch traced here: 817 us
  waiting for transfers between devices  197 us (24%)
  blocking collectives  183 us (22%)
  local copies, waits for them, and re-layouts  151 us (18%)
  other arithmetic  114 us (14%)
  matrix products  112 us (14%)
  starting transfers between devices  42.1 us (5%)
  between operations  17 us (2%)
    psum x1, waiting for transfers between devices, shards(): lax.psum(normed_two_part.astype(jnp.bfloat16), 'mp').astype(jnp.float32)  68.1 us
    psum x1, waiting for transfers between devices, shards(): lax.psum(feed_part.astype(jnp.bfloat16), 'mp').astype(jnp.float32)  65.6 us
    all_gather x1, waiting for transfers between devices, shards(): lax.all_gather(narrow_weight.astype(jnp.bfloat16), 'dp', axis=1, tiled=True)  39.3 us
    unnamed x155, local copies, waits for them, and re-layouts  36.8 us
    all_to_all x1, blocking collectives, summed_on_arrival(): parts = lax.all_to_all(cut_along(x, dim, size), axis, 0, 0, tiled=True)  34.1 us
    all_gather x1, blocking collectives, shards(): lax.all_gather(attend_weight.astype(jnp.bfloat16), 'dp', axis=0, tiled=True)  33.2 us
    all_gather x1, blocking collectives, shards(): lax.all_gather(project_weight.astype(jnp.bfloat16), 'dp', axis=1, tiled=T...  31.4 us
    all_gather x1, blocking collectives, shards(): lax.all_gather(heads_offset.astype(jnp.bfloat16), 'dp', axis=2, tiled=True)  30.6 us
  transfers between devices with their start and end apart: 11, of which 7 were waited for; matrix products, arithmetic and copies ran while one was open for 25% of the time, Pallas kernels for 0%

commit v1 on v0

--- a/solution.py
+++ b/solution.py
@@ -120,11 +120,36 @@
     hidden_second,
     vectors_second,
 ):
+
+    def _settle_halves(local_x):
+        mat_out = lax.axis_size("dp")
+        carry_in = lax.axis_index("dp")
+        reached, f_now, piece_out = (mat_out, carry_in, local_x.shape[1])
+        right_arr = tuple((ix * reached if b == 1 else ix for b, ix in enumerate(local_x.shape)))
+        reply = jnp.zeros(right_arr, local_x.dtype)
+        s_next = lax.dynamic_update_slice_in_dim(reply, local_x, f_now * piece_out, axis=1)
+        i0 = 1
+        work_now = tmp = local_x
+        while i0 < reached // 2 + 1:
+            state_now = tuple(((b, (b + 1) % reached) for b in range(reached)))
+            work_now = lax.ppermute(work_now, "dp", state_now)
+            s_next = lax.dynamic_update_slice_in_dim(
+                s_next, work_now, (f_now - i0) % reached * piece_out, axis=1
+            )
+            if 2 * i0 < reached:
+                then = tuple(((b, (b - 1) % reached) for b in range(reached)))
+                tmp = lax.ppermute(tmp, "dp", perm=then)
+                s_next = lax.dynamic_update_slice_in_dim(
+                    s_next, tmp, (f_now + i0) % reached * piece_out, axis=1
+                )
+            i0 = i0 + 1
+        return s_next
+
     fore_attend, fore_project, fore_widen, fore_narrow, fore_heads, fore_hidden, fore_vectors = (
         lax.all_gather(attend_weight.astype(jnp.bfloat16), "dp", axis=0, tiled=True),
         lax.all_gather(project_weight.astype(jnp.bfloat16), "dp", axis=1, tiled=True),
         lax.all_gather(widen_weight.astype(jnp.bfloat16), "dp", axis=0, tiled=True),
-        lax.all_gather(narrow_weight.astype(jnp.bfloat16), "dp", axis=1, tiled=True),
+        _settle_halves(narrow_weight.astype(jnp.bfloat16)),
         lax.all_gather(heads_offset.astype(jnp.bfloat16), "dp", axis=2, tiled=True),
         lax.all_gather(hidden_offset.astype(jnp.bfloat16), "dp", axis=1, tiled=True),
         lax.all_gather(layer_vectors.astype(jnp.bfloat16), "dp", axis=1, tiled=True),

time: 827 us -> 787 us (0.952)
  blocking collectives: 183 us -> 149 us
  waiting for transfers between devices: 197 us -> 167 us
  starting transfers between devices: 42.1 us -> 52.5 us
  local copies, waits for them, and re-layouts: 151 us -> 161 us
    all_gather x1 -> x0, waiting for transfers between devices: 39.3 us -> none  [shards(): lax.all_gather(narrow_weight.astype(jnp.bfloat16), 'dp', axis=1, tiled=True)]
    all_to_all x1 -> x0, blocking collectives: 34.1 us -> none  [summed_on_arrival(): parts = lax.all_to_all(cut_along(x, dim, size), axis, 0, 0, tiled=True)]
    all_to_all x6 -> x7, waiting for transfers between devices: 19.7 us -> 37.6 us  [summed_on_arrival(): parts = lax.all_to_all(cut_along(x, dim, size), axis, 0, 0, tiled=True)]
    ppermute x0 -> x7, starting transfers between devices: none -> 14.4 us  [the longest x3 13.6 us: _settle_halves(): tmp = lax.ppermute(tmp, 'dp', perm=then)]
    all_gather x1 -> x0, starting transfers between devices: 12.3 us -> none  [shards(): lax.all_gather(narrow_weight.astype(jnp.bfloat16), 'dp', axis=1, tiled=True)]
    psum x1, waiting for transfers between devices: 65.6 us -> 54.7 us  [shards(): lax.psum(feed_part.astype(jnp.bfloat16), 'mp').astype(jnp.float32)]
    ppermute x0 -> x7, waiting for transfers between devices: none -> 8.35 us  [the longest x4 8.34 us: _settle_halves(): work_now = lax.ppermute(work_now, 'dp', state_now)]
    all_to_all x6 -> x7, starting transfers between devices: 29.6 us -> 37.3 us  [summed_on_arrival(): parts = lax.all_to_all(cut_along(x, dim, size), axis, 0, 0, tiled=True)]
  transfers between devices with their start and end apart: 11 -> 18, of which waited for: 7 -> 7; matrix products, arithmetic and copies ran while one was open for 25% -> 29% of each run, Pallas kernels for 0% -> 0%
where the time goes in v1:
time: 787 us; the launch traced here: 778 us
  waiting for transfers between devices  167 us (21%)
  local copies, waits for them, and re-layouts  161 us (20%)
  blocking collectives  149 us (19%)
  other arithmetic  119 us (15%)
  matrix products  110 us (14%)
  starting transfers between devices  52.5 us (7%)
  between operations  17.4 us (2%)
    psum x1, waiting for transfers between devices, shards(): lax.psum(normed_two_part.astype(jnp.bfloat16), 'mp').astype(jnp.float32)  66.6 us
    psum x1, waiting for transfers between devices, shards(): lax.psum(feed_part.astype(jnp.bfloat16), 'mp').astype(jnp.float32)  54.7 us
    all_to_all x7, waiting for transfers between devices, summed_on_arrival(): parts = lax.all_to_all(cut_along(x, dim, size), axis, 0, 0, tiled=True)  37.6 us
    all_to_all x7, starting transfers between devices, summed_on_arrival(): parts = lax.all_to_all(cut_along(x, dim, size), axis, 0, 0, tiled=True)  37.3 us
    unnamed x151, local copies, waits for them, and re-layouts  36 us
    all_gather x1, blocking collectives, shards(): lax.all_gather(attend_weight.astype(jnp.bfloat16), 'dp', axis=0, tiled=True)  33.2 us
    all_gather x1, blocking collectives, shards(): lax.all_gather(project_weight.astype(jnp.bfloat16), 'dp', axis=1, tiled=T...  31.2 us
    all_gather x1, blocking collectives, shards(): lax.all_gather(heads_offset.astype(jnp.bfloat16), 'dp', axis=2, tiled=True)  30.6 us
  transfers between devices with their start and end apart: 18, of which 7 were waited for; matrix products, arithmetic and copies ran while one was open for 29% of the time, Pallas kernels for 0%

profile of v1, /device:TPU:0, one launch (start us, length us, event | category | flops | bytes accessed | tf_op | source)
XLA Modules:
  0.0 777.6 jit_solution(9186950316923443705)
XLA Ops:
  8.8 27.9 %all-gather = bf16[8,96,6]{1,2,0:T(8,128)(2,1)S(1)} all-gather(bf16[1,96,6]{1,2,0:T(8,128)(2,1)S(1)} %convert_bitcast_fusion), channel_id=1, replica_groups=mesh['dp'=8,'mp'=4] {'dp'}, dimensions={0}, use_global_device_ids=true | all-gather | bytes 10368 | tf_op jit(solution)/shard_map/all_gather | solution.py:155
  39.5 33.2 %all_gather.19 = bf16[768,3,192]{2,0,1:T(8,128)(2,1)S(1)} all-gather(bf16[96,3,192]{2,0,1:T(8,128)(2,1)S(1)} %convert_element_type.217), channel_id=1, replica_groups=mesh['dp'=8,'mp'=4] {'dp'}, dimensions={0}, use_global_device_ids=true | all-gather | bytes 995328 | tf_op jit(solution)/shard_map/all_gather | solution.py:149
  73.7 5.7 multiply_cosine_fusion.2
  79.4 19.3 %multiply_cosine_fusion = (f32[16,147,144]{2,0,1:T(8,128)S(1)}, f32[16,147,144]{2,0,1:T(8,128)}, f32[16,147,144]{2,0,1:T(8,128)}, f32[16,147,144]{2,0,1:T(8,128)}) fusion(f32[16,147]{0,1:T(8,128)S(1)} %copy.347, f32[144]{0:T(256)S(1)} %multiply_exponential_fusion, f32[16,147]{0,1:T(8,128)S(1)} %copy.346), kind=kLoop, calls=%fused_computation.60 | loop fusion | flops 677376 | bytes 5438400 | tf_op jit(solution)/shard_map/cos | solution.py:35
  98.7 11.6 %concatenate.5 = f32[16,147,768]{2,0,1:T(8,128)} concatenate(f32[16,147,96]{2,0,1:T(8,128)} %get-tuple-element.357, f32[16,147,96]{2,0,1:T(8,128)} %get-tuple-element.356, f32[16,147,144]{2,0,1:T(8,128)} %get-tuple-element.365, f32[16,147,144]{2,0,1:T(8,128)} %get-tuple-element.366, f32[16,147,144]{2,0,1:T(8,128)} %get-tuple-element.353, f32[16,147,144]{2,0,1:T(8,128)S(1)} %get-tuple-element.352), dimensions={2} | concatenate | bytes 14450688 | tf_op jit(solution)/shard_map/concatenate | solution.py:46
  110.3 7.8 %fusion.87 = (f32[16,147]{0,1:T(8,128)S(1)}, f32[16,147,768]{2,0,1:T(8,128)}) fusion(f32[16,147,768]{2,0,1:T(8,128)} %concatenate.5, bf16[16,147,768]{2,0,1:T(8,128)(2,1)} %param.25), kind=kLoop, calls=%fused_computation.195 | loop fusion | flops 5416656 | bytes 18072768 | tf_op jit(solution)/shard_map/reduce_sum | solution.py:57
  118.8 4.0 multiply_reduce_fusion.3
  123.0 3.8 add_convert_fusion.2
  126.8 3.1 copy.354
  129.9 3.9 reshape.315
  133.8 4.5 fusion.43
  140.6 30.6 %all_gather.20 = bf16[2,3,64]{1,0,2:T(2,128)(2,1)S(1)} all-gather(bf16[2,3,8]{1,0,2:T(2,128)(2,1)S(1)} %copy.356), channel_id=1, replica_groups=mesh['dp'=8,'mp'=4] {'dp'}, dimensions={2}, use_global_device_ids=true | all-gather | bytes 864 | tf_op jit(solution)/shard_map/all_gather | solution.py:153
  171.5 31.2 %all_gather.21 = bf16[192,768]{0,1:T(8,128)(2,1)S(1)} all-gather(bf16[192,96]{0,1:T(8,128)(2,1)S(1)} %copy.364), channel_id=1, replica_groups=mesh['dp'=8,'mp'=4] {'dp'}, dimensions={1}, use_global_device_ids=true | all-gather | bytes 331776 | tf_op jit(solution)/shard_map/all_gather | solution.py:150
  202.7 5.3 convert_element_type.222
  208.0 5.4 squeeze.10
  213.3 6.2 squeeze.11
  219.6 5.9 multiply_reduce_fusion.4
  228.4 3.1 fusion.30
  233.6 4.0 convert_element_type.226
  237.5 4.2 convolution_convert_fusion.2
  245.2 4.1 collective-permute-start.1
  251.5 10.3 %copy.348 = f32[16,147,768]{2,1,0:T(8,128)} copy(f32[16,147,768]{2,0,1:T(8,128)} %get-tuple-element.349) | data formatting | bytes 14450688 | tf_op jit(solution)/shard_map/add | solution.py:168
  262.5 26.4 %all_gather.23 = bf16[12,64]{0,1:T(8,128)(2,1)S(1)} all-gather(bf16[12,8]{0,1:T(8,128)(2,1)S(1)} %convert_element_type.232), channel_id=1, replica_groups=mesh['dp'=8,'mp'=4] {'dp'}, dimensions={1}, use_global_device_ids=true | all-gather | bytes 1728 | tf_op jit(solution)/shard_map/all_gather | solution.py:154
  292.3 6.2 copy.366
  298.4 5.6 reshape.304
  304.1 5.6 reshape.301
  309.7 4.7 collective-permute-start.3
  317.7 4.8 collective-permute-start.5
  327.1 6.5 collective-permute-done.6
  334.2 5.1 fusion.86
  345.1 20.1 %multiply_convert_fusion.2 = (bf16[2352,768]{1,0:T(8,128)(2,1)}, f32[2352,768]{1,0:T(8,128)S(1)}, f32[2352,768]{1,0:T(8,128)S(1)}) fusion(f32[768]{0:T(1024)} %reshape.311, bf16[2352,768]{1,0:T(8,128)(2,1)} %add_convert_fusion.1, bf16[768,768]{1,0:T(8,128)(2,1)} %all-gather.3.cloned.1.call-done), kind=kOutput, calls=%fused_computation.31 | convolution fusion | flops 2893750272 | bytes 22858752 | tf_op jit(solution)/shard_map/dot_general | solution.py:199
  365.2 8.8 %fusion.91 = (bf16[768]{0:T(1024)(128)(2,1)}, bf16[2352,768]{1,0:T(8,128)(2,1)S(1)}) fusion(f32[2352,768]{1,0:T(8,128)S(1)} %get-tuple-element.345, bf16[768,768]{0,1:T(8,128)(2,1)} %constant_dynamic-update-slice_fusion.6, f32[2352,768]{1,0:T(8,128)} %reshape.304, f32[2352]{0:T(1024)S(1)} %copy-done.26, f32[2352,768]{1,0:T(8,128)S(1)} %get-tuple-element.369, ...), kind=kOutput, calls=%fused_computation.199 | convolution fusion | flops 2807045376 | bytes 26482368 | tf_op jit(solution)/shard_map/dot_general | solution.py:77
  375.8 4.5 convolution_convert_fusion
  383.2 4.1 all-to-all-start.5
  387.3 66.6 %all-reduce.7.cloned.1.call-done = bf16[2352,768]{1,0:T(8,128)(2,1)} async-done(((bf16[2352,768]{1,0:T(8,128)(2,1)}), bf16[2352,768]{1,0:T(8,128)(2,1)}) %all-reduce.7.cloned.1.call-update) | async-done | bytes 3612688 | tf_op jit(solution)/shard_map/psum | solution.py:224
  453.9 7.8 fusion.10
  461.7 7.6 fusion.82
  469.3 3.0 copy-done.2
  474.6 6.2 reshape.305
  480.8 5.6 convolution_bitcast_fusion
  486.4 7.2 multiply_reduce_fusion
  512.6 3.5 fusion.84
  516.9 5.7 all-to-all-start.4
  522.6 7.4 convolution_convert_fusion.6
  530.0 6.0 all-to-all-start.2
  536.1 8.6 %convolution_convert_fusion.5 = bf16[768,768]{0,1:T(8,128)(2,1)} fusion(bf16[2352,768]{1,0:T(8,128)(2,1)} %get-tuple-element.344, f32[2352,768]{1,0:T(8,128)} %reshape.304, f32[2352]{0:T(1024)S(1)} %copy-done.28), kind=kOutput, calls=%fused_computation.83 | convolution fusion | flops 2778734592 | bytes 12027072 | tf_op jit(solution)/shard_map/dot_general | solution.py:71
  544.7 19.5 %all-to-all-done.2 = bf16[8,96,768]{2,1,0:T(8,128)(2,1)S(1)} async-done(((bf16[8,96,768]{2,1,0:T(8,128)(2,1)}), bf16[8,96,768]{2,1,0:T(8,128)(2,1)S(1)}, u32[]{:S(2)}, u32[]{:S(2)}) %all-to-all-start.2) | async-done | bytes 1179680 | tf_op jit(solution)/shard_map/all_to_all | solution.py:26
  564.1 3.6 all-to-all-start.3
  568.0 7.3 convolution_convert_fusion.1
  575.3 5.1 bitcast_convert_fusion
  594.7 4.8 fusion.40
  601.7 6.1 all-to-all-start.1
  607.9 6.3 fusion.31
  614.2 3.2 reshape.307
  620.0 6.0 all-to-all-start
  635.6 18.1 %all-to-all-done = bf16[8,96,3,192]{1,3,2,0:T(8,128)(2,1)} async-done(((bf16[8,96,3,192]{1,3,2,0:T(8,128)(2,1)}), bf16[8,96,3,192]{1,3,2,0:T(8,128)(2,1)}, u32[]{:S(2)}, u32[]{:S(2)}) %all-to-all-start) | async-done | bytes 884768 | tf_op jit(solution)/shard_map/all_to_all | solution.py:26
  661.3 54.7 %all-reduce.9.cloned.1.call-done = (bf16[2352,768]{1,0:T(8,128)(2,1)}, bf16[2352,768]{1,0:T(8,128)(2,1)}) async-done(((bf16[2352,768]{1,0:T(8,128)(2,1)}, bf16[2352,768]{1,0:T(8,128)(2,1)}), (bf16[2352,768]{1,0:T(8,128)(2,1)}, bf16[2352,768]{1,0:T(8,128)(2,1)})) %all-reduce.9.cloned.1.call-update) | async-done | bytes 7225360 | tf_op jit(solution)/shard_map/psum | solution.py:204
  718.7 7.2 fusion.15
  726.7 5.8 all-to-all-start.6
  732.6 11.5 %fusion.13 = f32[2352,768]{1,0:T(8,128)} fusion(f32[2352,768]{1,0:T(8,128)} %copy-done.2, bf16[2352,768]{1,0:T(8,128)(2,1)} %get-tuple-element.309, f32[2352,768]{1,0:T(8,128)} %reshape.301, f32[2352]{0:T(1024)S(1)} %broadcast_multiply_fusion.1, f32[2352]{0:T(1024)S(1)} %div.112, f32[2352]{0:T(1024)S(1)} %broadcast_multiply_fusion.2, f32[768]{0:T(1024)S(1)} %copy-done.31, ...), kind=kLoop, calls=%fused_computation.22 | loop fusion | flops 16257024 | bytes 25329408 | tf_op jit(solution)/shard_map/add | solution.py:269
  746.9 3.8 reshape.303
  750.8 4.6 copy.395
  755.3 5.4 reshape.306
  760.8 8.5 %copy.396 = f32[16,147,768]{2,0,1:T(8,128)} copy(f32[16,147,768]{2,1,0:T(8,128)} %reshape.306) | data formatting | bytes 14450688
  (273 shorter events, 106.0 us)
Async XLA Ops:
  8.0 326.2 %all-reduce.5.cloned.1.call-start = ((), (), s32[]{:S(2)}) async-start(), calls=%async_computation.7 | async-start | bytes 7225344 | tf_op jit(solution)/shard_map/psum | solution.py:195
  37.5 85.5 %copy-start.30 = (f32[768]{0:T(1024)}, f32[768]{0:T(1024)S(1)}, u32[]{:S(2)}) copy-start(f32[768]{0:T(1024)S(1)} %get-tuple-element.307) | copy-start | bytes 9220
  122.9 7.0 copy-start.24
  138.3 33.1 %copy-start.17 = (f32[192,96]{1,0:T(8,128)S(1)}, f32[192,96]{1,0:T(8,128)}, u32[]{:S(2)}) copy-start(f32[192,96]{1,0:T(8,128)} %param.30) | copy-start | bytes 221188
  171.3 55.9 %copy-start.35 = (f32[1,3,64]{2,1,0:T(4,128)}, f32[1,3,64]{2,1,0:T(4,128)S(1)}, u32[]{:S(2)}) copy-start(f32[1,3,64]{2,1,0:T(4,128)S(1)} %copy.357) | copy-start | bytes 2308
  171.4 54.1 %copy-start.33 = (f32[1,3,64]{2,1,0:T(4,128)}, f32[1,3,64]{2,1,0:T(4,128)S(1)}, u32[]{:S(2)}) copy-start(f32[1,3,64]{2,1,0:T(4,128)S(1)} %copy.359) | copy-start | bytes 2308
  225.5 6.0 copy-start
  241.7 103.4 %all-gather.3.cloned.1.call-start = ((), (), s32[]{:S(2)}) async-start(), calls=%async_computation.8 | async-start | bytes 1327104 | tf_op jit(solution)/shard_map/all_gather | solution.py:151
  244.6 65.1 %collective-permute-start = (bf16[768,96]{0,1:T(8,128)(2,1)}, bf16[768,96]{0,1:T(8,128)(2,1)}, u32[]{:S(2)}, u32[]{:S(2)}) collective-permute-start(bf16[768,96]{0,1:T(8,128)(2,1)} %get-tuple-element.343), channel_id=1, source_target_pairs={{0,4},{4,8},{8,12},{12,16},{16,20},{20,24},{24,28},{28,0},{1,5},{5... | collective-permute-start | bytes 442376 | tf_op jit(solution)/shard_map/ppermute | solution.py:135
  245.2 64.4 %collective-permute-start.1 = (bf16[768,96]{0,1:T(8,128)(2,1)}, bf16[768,96]{0,1:T(8,128)(2,1)}, u32[]{:S(2)}, u32[]{:S(2)}) collective-permute-start(bf16[768,96]{0,1:T(8,128)(2,1)} %get-tuple-element.343), channel_id=1, source_target_pairs={{0,28},{4,0},{8,4},{12,8},{16,12},{20,16},{24,20},{28,24},{1,29},{... | collective-permute-start | bytes 442376 | tf_op jit(solution)/shard_map/ppermute | solution.py:141
  251.0 203.0 %all-reduce.7.cloned.1.call-start = ((), (), s32[]{:S(2)}) async-start(), calls=%async_computation.9 | async-start | bytes 7225344 | tf_op jit(solution)/shard_map/psum | solution.py:224
  251.5 11.0 %copy-start.42 = (f32[12,8]{0,1:T(8,128)S(1)}, f32[12,8]{0,1:T(8,128)}, u32[]{:S(2)}) copy-start(f32[12,8]{0,1:T(8,128)} %param.34) | copy-start | bytes 1156
  304.1 30.2 %copy-start.39 = (f32[768]{0:T(1024)S(1)}, f32[768]{0:T(1024)}, u32[]{:S(2)}) copy-start(f32[768]{0:T(1024)} %get-tuple-element.305) | copy-start | bytes 9220
  309.7 8.1 %collective-permute-start.2 = (bf16[768,96]{0,1:T(8,128)(2,1)}, bf16[768,96]{0,1:T(8,128)(2,1)S(1)}, u32[]{:S(2)}, u32[]{:S(2)}) collective-permute-start(bf16[768,96]{0,1:T(8,128)(2,1)} %collective-permute-done), channel_id=1, source_target_pairs={{0,4},{4,8},{8,12},{12,16},{16,20},{20,24},{24,28},{28,0},{1,5},{5... | collective-permute-start | bytes 442376 | tf_op jit(solution)/shard_map/ppermute | solution.py:135
  309.7 8.0 %collective-permute-start.3 = (bf16[768,96]{0,1:T(8,128)(2,1)}, bf16[768,96]{0,1:T(8,128)(2,1)S(1)}, u32[]{:S(2)}, u32[]{:S(2)}) collective-permute-start(bf16[768,96]{0,1:T(8,128)(2,1)} %collective-permute-done.1), channel_id=1, source_target_pairs={{0,28},{4,0},{8,4},{12,8},{16,12},{20,16},{24,20},{28,24},{1,29},{... | collective-permute-start | bytes 442376 | tf_op jit(solution)/shard_map/ppermute | solution.py:141
  317.7 7.8 %collective-permute-start.4 = (bf16[768,96]{0,1:T(8,128)(2,1)S(1)}, bf16[768,96]{0,1:T(8,128)(2,1)S(1)}, u32[]{:S(2)}, u32[]{:S(2)}) collective-permute-start(bf16[768,96]{0,1:T(8,128)(2,1)S(1)} %collective-permute-done.2), channel_id=1, source_target_pairs={{0,4},{4,8},{8,12},{12,16},{16,20},{20,24},{24,28},{28,0},{1,5},{5... | collective-permute-start | bytes 442376 | tf_op jit(solution)/shard_map/ppermute | solution.py:135
  317.7 8.7 %collective-permute-start.5 = (bf16[768,96]{0,1:T(8,128)(2,1)S(1)}, bf16[768,96]{0,1:T(8,128)(2,1)S(1)}, u32[]{:S(2)}, u32[]{:S(2)}) collective-permute-start(bf16[768,96]{0,1:T(8,128)(2,1)S(1)} %collective-permute-done.3), channel_id=1, source_target_pairs={{0,28},{4,0},{8,4},{12,8},{16,12},{20,16},{24,20},{28,24},{1,29},{... | collective-permute-start | bytes 442376 | tf_op jit(solution)/shard_map/ppermute | solution.py:141
  325.6 8.0 %collective-permute-start.6 = (bf16[768,96]{0,1:T(8,128)(2,1)S(1)}, bf16[768,96]{0,1:T(8,128)(2,1)S(1)}, u32[]{:S(2)}, u32[]{:S(2)}) collective-permute-start(bf16[768,96]{0,1:T(8,128)(2,1)S(1)} %collective-permute-done.4), channel_id=1, source_target_pairs={{0,4},{4,8},{8,12},{12,16},{16,20},{20,24},{24,28},{28,0},{1,5},{5... | collective-permute-start | bytes 442376 | tf_op jit(solution)/shard_map/ppermute | solution.py:135
  345.1 20.1 %copy-start.26 = (f32[2352]{0:T(1024)S(1)}, f32[2352]{0:T(1024)}, u32[]{:S(2)}) copy-start(f32[2352]{0:T(1024)} %mul.476) | copy-start | bytes 28228
  345.1 20.1 %copy-start.54 = (f32[768]{0:T(1024)S(1)}, f32[768]{0:T(1024)}, u32[]{:S(2)}) copy-start(f32[768]{0:T(1024)} %reshape.311) | copy-start | bytes 9220
  365.2 10.6 %copy-start.59 = (bf16[768,768]{1,0:T(8,128)(2,1)S(1)}, bf16[768,768]{1,0:T(8,128)(2,1)}, u32[]{:S(2)}) copy-start(bf16[768,768]{1,0:T(8,128)(2,1)} %all-gather.3.cloned.1.call-done) | copy-start | bytes 3538948
  383.2 133.7 %all-to-all-start.5 = ((bf16[8,12,8]{1,2,0:T(8,128)(2,1)}), bf16[8,12,8]{1,2,0:T(8,128)(2,1)}, u32[]{:S(2)}, u32[]{:S(2)}) async-start(bf16[8,12,8]{1,2,0:T(8,128)(2,1)} %copy.382), calls=%async_computation.5 | async-start | bytes 32768 | tf_op jit(solution)/shard_map/all_to_all | solution.py:26
  453.9 7.8 copy-start.3
  453.9 7.8 copy-start.21
  453.9 7.8 %copy-start.27 = (f32[2352]{0:T(1024)S(1)}, f32[2352]{0:T(1024)}, u32[]{:S(2)}) copy-start(f32[2352]{0:T(1024)} %mul.476) | copy-start | bytes 28228
  474.6 11.8 %copy-start.13 = (f32[16,3,147]{2,1,0:T(4,128)S(1)}, f32[16,3,147]{2,1,0:T(4,128)}, u32[]{:S(2)}) copy-start(f32[16,3,147]{2,1,0:T(4,128)} %copy-done.12) | copy-start | bytes 84676
  474.6 11.8 %copy-start.36 = (f32[1,3,64]{2,1,0:T(4,128)S(1)}, f32[1,3,64]{2,1,0:T(4,128)}, u32[]{:S(2)}) copy-start(f32[1,3,64]{2,1,0:T(4,128)} %copy-done.35) | copy-start | bytes 2308
  480.8 5.7 copy-start.6
  480.8 12.9 %slice-start = ((s8[7471104]{0:T(1024)(128)(4,1)}), s8[4194304]{0:T(1024)(128)(4,1)S(1)}, s32[]{:S(2)}) async-start(s8[7471104]{0:T(1024)(128)(4,1)} %bitcast.93), calls=%async_computation.11 | async-start | bytes 8388608
  486.4 7.3 slice-start.1
  516.9 13.2 %all-to-all-start.4 = ((bf16[8,2,3,8]{3,1,2,0:T(2,128)(2,1)}), bf16[8,2,3,8]{3,1,2,0:T(2,128)(2,1)S(1)}, u32[]{:S(2)}, u32[]{:S(2)}) async-start(bf16[8,2,3,8]{3,1,2,0:T(2,128)(2,1)} %copy.379), calls=%async_computation.4 | async-start | bytes 24576 | tf_op jit(solution)/shard_map/all_to_all | solution.py:26
  522.6 13.4 %copy-start.28 = (f32[2352]{0:T(1024)S(1)}, f32[2352]{0:T(1024)}, u32[]{:S(2)}) copy-start(f32[2352]{0:T(1024)} %mul.476) | copy-start | bytes 28228
  530.0 34.1 %all-to-all-start.2 = ((bf16[8,96,768]{2,1,0:T(8,128)(2,1)}), bf16[8,96,768]{2,1,0:T(8,128)(2,1)S(1)}, u32[]{:S(2)}, u32[]{:S(2)}) async-start(bf16[8,96,768]{2,1,0:T(8,128)(2,1)} %bitcast.18), calls=%async_computation.2 | async-start | bytes 2359296 | tf_op jit(solution)/shard_map/all_to_all | solution.py:26
  564.1 37.6 %all-to-all-start.3 = ((bf16[8,768,96]{1,2,0:T(8,128)(2,1)}), bf16[8,768,96]{1,2,0:T(8,128)(2,1)S(1)}, u32[]{:S(2)}, u32[]{:S(2)}) async-start(bf16[8,768,96]{1,2,0:T(8,128)(2,1)} %bitcast.97), calls=%async_computation.3 | async-start | bytes 2359296 | tf_op jit(solution)/shard_map/all_to_all | solution.py:26
  567.7 148.3 %all-reduce.9.cloned.1.call-start = ((), (), s32[]{:S(2)}) async-start(), calls=%async_computation.10 | async-start | bytes 14450688 | tf_op jit(solution)/shard_map/psum | solution.py:204
  568.0 7.3 copy-start.9
  568.0 7.3 copy-start.11
  580.3 10.2 %copy-start.43 = (f32[12,8]{0,1:T(8,128)S(1)}, f32[12,8]{0,1:T(8,128)}, u32[]{:S(2)}) copy-start(f32[12,8]{0,1:T(8,128)} %param.34) | copy-start | bytes 1156
  580.3 10.2 %copy-start.50 = (f32[12,8]{0,1:T(8,128)S(1)}, f32[12,8]{0,1:T(8,128)}, u32[]{:S(2)}) copy-start(f32[12,8]{0,1:T(8,128)} %param.41) | copy-start | bytes 1156
  580.4 10.2 %copy-start.51 = (f32[12,8]{0,1:T(8,128)S(1)}, f32[12,8]{0,1:T(8,128)}, u32[]{:S(2)}) copy-start(f32[12,8]{0,1:T(8,128)} %param.48) | copy-start | bytes 1156
  580.4 13.5 %copy-start.47 = (bf16[768]{0:T(1024)(128)(2,1)S(1)}, bf16[768]{0:T(1024)(128)(2,1)}, u32[]{:S(2)}) copy-start(bf16[768]{0:T(1024)(128)(2,1)} %get-tuple-element.296) | copy-start | bytes 4612
  580.4 14.2 %copy-start.49 = (bf16[768]{0:T(1024)(128)(2,1)S(1)}, bf16[768]{0:T(1024)(128)(2,1)}, u32[]{:S(2)}) copy-start(bf16[768]{0:T(1024)(128)(2,1)} %get-tuple-element.338) | copy-start | bytes 4612
  580.4 14.3 %copy-start.7 = (bf16[2352,192]{0,1:T(8,128)(2,1)S(1)}, bf16[2352,192]{0,1:T(8,128)(2,1)}, u32[]{:S(2)}) copy-start(bf16[2352,192]{0,1:T(8,128)(2,1)} %convert_element_type.226) | copy-start | bytes 2709508
  590.6 23.6 %copy-start.40 = (f32[12,8]{0,1:T(8,128)}, f32[12,8]{0,1:T(8,128)S(1)}, u32[]{:S(2)}) copy-start(f32[12,8]{0,1:T(8,128)S(1)} %convert_reduce_fusion.5) | copy-start | bytes 1156
  601.7 18.3 %all-to-all-start.1 = ((bf16[8,192,96]{2,1,0:T(8,128)(2,1)}), bf16[8,192,96]{2,1,0:T(8,128)(2,1)S(1)}, u32[]{:S(2)}, u32[]{:S(2)}) async-start(bf16[8,192,96]{2,1,0:T(8,128)(2,1)} %bitcast.91), calls=%async_computation.1 | async-start | bytes 786432 | tf_op jit(solution)/shard_map/all_to_all | solution.py:26
  607.8 18.8 %copy-start.46 = (f32[2,3,8]{2,0,1:T(2,128)S(1)}, f32[2,3,8]{2,0,1:T(2,128)}, u32[]{:S(2)}) copy-start(f32[2,3,8]{2,0,1:T(2,128)} %param.33) | copy-start | bytes 580
  607.9 18.8 %copy-start.55 = (f32[2,3,8]{2,0,1:T(2,128)S(1)}, f32[2,3,8]{2,0,1:T(2,128)}, u32[]{:S(2)}) copy-start(f32[2,3,8]{2,0,1:T(2,128)} %param.40) | copy-start | bytes 580
  607.9 18.8 %copy-start.56 = (f32[2,3,8]{2,0,1:T(2,128)S(1)}, f32[2,3,8]{2,0,1:T(2,128)}, u32[]{:S(2)}) copy-start(f32[2,3,8]{2,0,1:T(2,128)} %param.47) | copy-start | bytes 580
  614.2 15.1 %copy-start.14 = (f32[96,768]{1,0:T(8,128)S(1)}, f32[96,768]{1,0:T(8,128)}, u32[]{:S(2)}) copy-start(f32[96,768]{1,0:T(8,128)} %param.31) | copy-start | bytes 884740
  614.2 19.7 %copy-start.18 = (f32[192,96]{1,0:T(8,128)S(1)}, f32[192,96]{1,0:T(8,128)}, u32[]{:S(2)}) copy-start(f32[192,96]{1,0:T(8,128)} %param.30) | copy-start | bytes 221188
  614.2 19.7 %copy-start.29 = (f32[192,96]{1,0:T(8,128)S(1)}, f32[192,96]{1,0:T(8,128)}, u32[]{:S(2)}) copy-start(f32[192,96]{1,0:T(8,128)} %param.37) | copy-start | bytes 221188
  620.0 33.8 %all-to-all-start = ((bf16[8,96,3,192]{1,3,2,0:T(8,128)(2,1)}), bf16[8,96,3,192]{1,3,2,0:T(8,128)(2,1)}, u32[]{:S(2)}, u32[]{:S(2)}) async-start(bf16[8,96,3,192]{1,3,2,0:T(8,128)(2,1)} %copy.376), calls=%async_computation | async-start | bytes 2359296 | tf_op jit(solution)/shard_map/all_to_all | solution.py:26
  629.3 26.2 %copy-start.16 = (f32[768,96]{0,1:T(8,128)}, f32[768,96]{0,1:T(8,128)S(1)}, u32[]{:S(2)}) copy-start(f32[768,96]{0,1:T(8,128)S(1)} %convert_reduce_fusion) | copy-start | bytes 884740
  631.6 87.1 %copy-start.31 = (f32[768]{0:T(1024)S(1)}, f32[768]{0:T(1024)}, u32[]{:S(2)}) copy-start(f32[768]{0:T(1024)} %copy-done.30) | copy-start | bytes 9220
  633.9 92.0 %copy-start.19 = (f32[192,96]{1,0:T(8,128)}, f32[192,96]{1,0:T(8,128)S(1)}, u32[]{:S(2)}) copy-start(f32[192,96]{1,0:T(8,128)S(1)} %convert_reduce_fusion.3) | copy-start | bytes 221188
  716.0 10.1 %copy-start.48 = (bf16[1,8,96]{2,1,0:T(8,128)(2,1)S(1)}, bf16[1,8,96]{2,1,0:T(8,128)(2,1)}, u32[]{:S(2)}) copy-start(bf16[1,8,96]{2,1,0:T(8,128)(2,1)} %stack.32) | copy-start | bytes 4612
  718.7 25.4 %slice-start.2 = ((s8[7225344]{0:T(1024)(128)(4,1)}), s8[3031040]{0:T(1024)(128)(4,1)S(1)}, s32[]{:S(2)}) async-start(s8[7225344]{0:T(1024)(128)(4,1)} %bitcast.95), calls=%async_computation.13 | async-start | bytes 6062080
  726.7 42.6 %all-to-all-start.6 = ((bf16[8,6,96]{2,1,0:T(8,128)(2,1)}), bf16[8,6,96]{2,1,0:T(8,128)(2,1)S(1)}, u32[]{:S(2)}, u32[]{:S(2)}) async-start(bf16[8,6,96]{2,1,0:T(8,128)(2,1)} %copy.384), calls=%async_computation.6 | async-start | bytes 32768 | tf_op jit(solution)/shard_map/all_to_all | solution.py:26
  732.6 11.5 %slice-start.3 = ((s8[7225344]{0:T(1024)(128)(4,1)}), s8[4194304]{0:T(1024)(128)(4,1)S(1)}, s32[]{:S(2)}) async-start(s8[7225344]{0:T(1024)(128)(4,1)} %bitcast.95), calls=%async_computation.14 | async-start | bytes 8388608
  732.6 11.5 %copy-start.10 = (bf16[2352,768]{1,0:T(8,128)(2,1)S(1)}, bf16[2352,768]{1,0:T(8,128)(2,1)}, u32[]{:S(2)}) copy-start(bf16[2352,768]{1,0:T(8,128)(2,1)} %get-tuple-element.308) | copy-start | bytes 10838020
  732.6 11.5 %copy-start.37 = (f32[768]{0:T(1024)S(1)}, f32[768]{0:T(1024)}, u32[]{:S(2)}) copy-start(f32[768]{0:T(1024)} %get-tuple-element.302) | copy-start | bytes 9220
  760.8 8.5 %copy-start.44 = (f32[6,96]{1,0:T(8,128)S(1)}, f32[6,96]{1,0:T(8,128)}, u32[]{:S(2)}) copy-start(f32[6,96]{1,0:T(8,128)} %param.35) | copy-start | bytes 6916
  760.8 8.5 %copy-start.52 = (f32[6,96]{1,0:T(8,128)S(1)}, f32[6,96]{1,0:T(8,128)}, u32[]{:S(2)}) copy-start(f32[6,96]{1,0:T(8,128)} %param.42) | copy-start | bytes 6916
  760.8 8.5 %copy-start.53 = (f32[6,96]{1,0:T(8,128)S(1)}, f32[6,96]{1,0:T(8,128)}, u32[]{:S(2)}) copy-start(f32[6,96]{1,0:T(8,128)} %param.49) | copy-start | bytes 6916
  (19 other events, 44.7 us)
Sparse Core Ops, SparseCore 0:
  241.8 76.3 all-reduce.4
  380.5 73.4 all-reduce.6
  580.5 135.4 all-reduce.8
Sparse Core Ops, SparseCore 1:
  251.0 38.5 all-gather.2
